TPU v7x, 32 devices: a whole 2x2x4 slice. The times are simulated.
32 devices in a mesh: seq: 4 (over x, core), chan: 8 (over z, y).
Axes of the slice: x: 2, y: 2, z: 4, core: 2. Of those that a mesh axis runs over, the one named last changes fastest.
Arguments:
- features: bfloat16 [3, 4096, 512], P(None, 'chan', 'seq'), may hold values from -6 to 6
- cotangent: bfloat16 [4096, 512], P('chan', 'seq'), may hold values from -6 to 6
- long_filter: bfloat16 [4096, 512], P('chan', 'seq'), may hold values from -0.25 to 0.25
- short_filters: float32 [3, 4096, 3], P(None, 'chan'), may hold values from -3.5 to 3.5
- skip_gain: float32 [4096], P('chan'), may hold values from -4 to 4
Outputs:
- gated_out: bfloat16 [4096, 512], P('chan', 'seq')
- feature_grad: bfloat16 [3, 4096, 512], P(None, 'chan', 'seq')
- long_grad: bfloat16 [4096, 512], P('chan', 'seq')
- short_grad: float32 [3, 4096, 3], P(None, 'chan')
- skip_grad: float32 [4096], P('chan')
All inputs are finite; a program needn't handle non-finite values.
Results may differ from a plain program's by a relative error of at most 0.015.
Values may be sent and summed in bfloat16 or wider, within the bound.
A program may use at most 64 MiB of HBM per device.

v0:
```python
import math
import jax
import jax.numpy as jnp
from jax import lax
from jax.sharding import PartitionSpec as P

inner_length = 128
radix_width = 8


def phase_tables(row_count, col_count, length, direction):
    phase_index = (
        lax.iota(jnp.int32, row_count)[:, None] * lax.iota(jnp.int32, col_count)[None, :] % length
    )
    angles = direction * 2.0 * math.pi / length * phase_index.astype(jnp.float32)
    return (jnp.cos(angles), jnp.sin(angles))


def last_axis(operand, matrix):
    return jnp.einsum("...n,nk->...k", operand, matrix, precision=lax.Precision.HIGH)


def first_axis(operand, matrix):
    return jnp.einsum("...ab,ak->...kb", operand, matrix, precision=lax.Precision.HIGH)


def transform(real_part, imag_part, direction):
    length = real_part.shape[-1]
    if length <= inner_length or length % radix_width != 0:
        cos_table, sin_table = phase_tables(length, length, length, direction)
        return (
            last_axis(real_part, cos_table) - last_axis(imag_part, sin_table),
            last_axis(real_part, sin_table) + last_axis(imag_part, cos_table),
        )
    rest_length = length // radix_width
    grid_shape = real_part.shape[:-1] + (radix_width, rest_length)
    real_grid = real_part.reshape(grid_shape)
    imag_grid = imag_part.reshape(grid_shape)
    cos_table, sin_table = phase_tables(radix_width, radix_width, radix_width, direction)
    section_real = first_axis(real_grid, cos_table) - first_axis(imag_grid, sin_table)
    section_imag = first_axis(real_grid, sin_table) + first_axis(imag_grid, cos_table)
    twist_cos, twist_sin = phase_tables(radix_width, rest_length, length, direction)
    turned_real = section_real * twist_cos - section_imag * twist_sin
    turned_imag = section_real * twist_sin + section_imag * twist_cos
    inner_real, inner_imag = transform(turned_real, turned_imag, direction)
    return (
        jnp.swapaxes(inner_real, -1, -2).reshape(real_part.shape),
        jnp.swapaxes(inner_imag, -1, -2).reshape(real_part.shape),
    )


def spectral(mixed_term, gated_grad, kernel, local_gain):
    length = mixed_term.shape[-1]
    mixed_wide = mixed_term.astype(jnp.float32)
    gated_wide = gated_grad.astype(jnp.float32)
    kernel_wide = kernel.astype(jnp.float32)
    extend = ((0, 0), (0, length))
    real_in = jnp.stack([jnp.pad(mixed_wide, extend), jnp.pad(kernel_wide, extend)])
    imag_in = jnp.stack(
        [jnp.pad(gated_wide, extend), jnp.zeros((kernel_wide.shape[0], 2 * length), jnp.float32)]
    )
    freq_real, freq_imag = transform(real_in, imag_in, -1.0)
    packed_real = freq_real[0]
    packed_imag = freq_imag[0]
    mirror_real = jnp.roll(jnp.flip(packed_real, -1), 1, -1)
    mirror_imag = jnp.roll(jnp.flip(packed_imag, -1), 1, -1)
    mix_real = 0.5 * (packed_real + mirror_real)
    mix_imag = 0.5 * (packed_imag - mirror_imag)
    grad_real = 0.5 * (packed_imag + mirror_imag)
    grad_imag = 0.5 * (mirror_real - packed_real)
    kern_real = freq_real[1]
    kern_imag = freq_imag[1]
    conv_real = mix_real * kern_real - mix_imag * kern_imag
    conv_imag = mix_real * kern_imag + mix_imag * kern_real
    corr_real = grad_real * kern_real + grad_imag * kern_imag
    corr_imag = grad_imag * kern_real - grad_real * kern_imag
    cross_real = grad_real * mix_real + grad_imag * mix_imag
    cross_imag = grad_imag * mix_real - grad_real * mix_imag
    back_real = jnp.stack([conv_real - corr_imag, cross_real])
    back_imag = jnp.stack([conv_imag + corr_real, cross_imag])
    time_real, time_imag = transform(back_real, back_imag, 1.0)
    inverse_scale = 1.0 / (2 * length)
    conv_part = time_real[0, :, :length] * inverse_scale
    corr_part = time_imag[0, :, :length] * inverse_scale
    cross_part = time_real[1, :, :length] * inverse_scale
    gain_column = local_gain[:, None]
    long_out = (conv_part + gain_column * mixed_wide).astype(jnp.bfloat16)
    mixed_grad = (corr_part + gain_column * gated_wide).astype(jnp.bfloat16)
    return (long_out, mixed_grad, cross_part.astype(jnp.bfloat16))


def featurize(history, weights, margin, span_count):
    running = weights[:, :, 0:1] * history[:, :, margin : margin + span_count]
    for offset in range(1, margin + 1):
        running = (
            running
            + weights[:, :, offset : offset + 1]
            * history[:, :, margin - offset : margin - offset + span_count]
        )
    return running


def unfeaturize(padded_grad, weights, span_count):
    running = weights[:, :, 0:1] * padded_grad[:, :, 0:span_count]
    for offset in range(1, weights.shape[2]):
        running = (
            running
            + weights[:, :, offset : offset + 1] * padded_grad[:, :, offset : offset + span_count]
        )
    return running


def tap_grads(primed_grad, history, margin, span_count):
    columns = []
    for offset in range(margin + 1):
        columns.append(
            jnp.sum(
                primed_grad * history[:, :, margin - offset : margin - offset + span_count], axis=-1
            )
        )
    return jnp.stack(columns, axis=-1)


def shards(features, cotangent, long_filter, short_filters, skip_gain):
    groups = lax.axis_size("seq")
    seq_index = lax.axis_index("seq")
    channels = features.shape[1]
    per_group = channels // groups
    margin = short_filters.shape[2] - 1
    local_gain = lax.dynamic_slice_in_dim(skip_gain, seq_index * per_group, per_group, 0)
    stacked = jnp.concatenate([features, cotangent[None], long_filter[None]], 0)
    columns = lax.all_to_all(stacked, "seq", split_axis=1, concat_axis=2, tiled=True)
    weights = lax.dynamic_slice_in_dim(short_filters, seq_index * per_group, per_group, 1)
    length = columns.shape[2]
    history = jnp.pad(columns[:3].astype(jnp.float32), ((0, 0), (0, 0), (margin, 0)))
    primed = featurize(history, weights, margin, length)
    mixed_term = (primed[1] * primed[2]).astype(jnp.bfloat16)
    cot_wide = columns[3].astype(jnp.float32)
    gated_grad = (cot_wide * primed[0]).astype(jnp.bfloat16)
    long_out, mixed_grad, kernel_grad = spectral(mixed_term, gated_grad, columns[4], local_gain)
    long_wide = long_out.astype(jnp.float32)
    mixed_back = mixed_grad.astype(jnp.float32)
    gated_out = (primed[0] * long_wide).astype(jnp.bfloat16)
    primed_grad = jnp.stack([cot_wide * long_wide, mixed_back * primed[2], mixed_back * primed[1]])
    padded_grad = jnp.pad(primed_grad, ((0, 0), (0, 0), (0, margin)))
    feature_grad = unfeaturize(padded_grad, weights, length).astype(jnp.bfloat16)
    taps_grad = tap_grads(primed_grad, history, margin, length)
    gain_grad = jnp.sum(gated_grad.astype(jnp.float32) * mixed_term.astype(jnp.float32), axis=-1)
    results = jnp.concatenate([gated_out[None], feature_grad, kernel_grad[None]], 0)
    row_blocks = lax.all_to_all(results, "seq", split_axis=2, concat_axis=1, tiled=True)
    short_grad, skip_grad = (
        lax.all_gather(taps_grad, "seq", axis=1, tiled=True),
        lax.all_gather(gain_grad, "seq", axis=0, tiled=True),
    )
    return (row_blocks[0], row_blocks[1:4], row_blocks[4], short_grad, skip_grad)


def solution(mesh):
    placed = (
        P(None, "chan", "seq"),
        P("chan", "seq"),
        P("chan", "seq"),
        P(None, "chan", None),
        P("chan"),
    )
    return jax.shard_map(
        shards,
        mesh=mesh,
        in_specs=placed,
        out_specs=(
            P("chan", "seq"),
            P(None, "chan", "seq"),
            P("chan", "seq"),
            P(None, "chan", None),
            P("chan"),
        ),
        check_vma=False,
    )
```

profile of v0, /device:TPU:0, one launch (start us, length us, event | category | flops | bytes accessed | tf_op | source)
XLA Modules:
  0.0 104.6 jit_solution(2643128398959037245)
XLA Ops:
  0.6 1.2 %copy.108 = bf16[1,512,128]{2,0,1:T(2,128)(2,1)S(1)} copy(bf16[1,512,128]{2,1,0:T(8,128)(2,1)} %bitcast.192) | data formatting | bytes 262144 | tf_op jit(solution)/shard_map/broadcast_in_dim | solution.py:131
  1.8 1.1 %copy.107 = bf16[1,512,128]{2,0,1:T(2,128)(2,1)S(1)} copy(bf16[1,512,128]{2,1,0:T(8,128)(2,1)} %bitcast.193) | data formatting | bytes 262144 | tf_op jit(solution)/shard_map/broadcast_in_dim | solution.py:131
  2.9 0.3 copy.106
  3.3 1.9 %pad_maximum_fusion = bf16[5,512,128]{2,0,1:T(8,128)(2,1)} fusion(bf16[1,512,128]{2,0,1:T(2,128)(2,1)S(1)} %copy.108, bf16[1,512,128]{2,0,1:T(2,128)(2,1)S(1)} %copy.107, bf16[3,512,128]{2,0,1:T(4,128)(2,1)S(1)} %copy.106), kind=kLoop, calls=%fused_computation.12 | loop fusion | flops 1966080 | bytes 1310720 | tf_op jit(solution)/shard_map/concatenate | solution.py:131
  5.1 4.2 %all-to-all-start = ((bf16[5,512,128]{2,0,1:T(8,128)(2,1)}), bf16[5,512,128]{2,0,1:T(8,128)(2,1)S(1)}, u32[]{:S(2)}, u32[]{:S(2)}) async-start(bf16[5,512,128]{2,0,1:T(8,128)(2,1)} %pad_maximum_fusion), calls=%async_computation | async-start | bytes 2097152 | tf_op jit(solution)/shard_map/all_to_all | solution.py:132
  9.4 0.9 constant_dynamic-slice_fusion.1
  10.3 1.3 %dynamic_slice.7 = f32[128]{0:T(128)} dynamic-slice(f32[512]{0:T(512)} %param.9, s32[]{:T(128)S(6)} %select_n.84), dynamic_slice_sizes={128} | dynamic-slice | bytes 1028 | tf_op jit(solution)/shard_map/dynamic_slice | solution.py:130
  11.6 0.7 multiply_sine_fusion.7
  12.3 0.6 multiply_sine_fusion.6
  12.9 10.9 %all-to-all-done = bf16[5,512,128]{2,0,1:T(8,128)(2,1)S(1)} async-done(((bf16[5,512,128]{2,0,1:T(8,128)(2,1)}), bf16[5,512,128]{2,0,1:T(8,128)(2,1)S(1)}, u32[]{:S(2)}, u32[]{:S(2)}) %all-to-all-start) | async-done | bytes 655392 | tf_op jit(solution)/shard_map/all_to_all | solution.py:132
  23.8 0.7 copy.109
  24.7 0.6 copy-done.1
  25.7 1.3 %multiply_reduce_fusion.2 = (f32[128]{0:T(128)}, f32[128,512]{0,1:T(8,128)}, bf16[1,128,512]{1,2,0:T(8,128)(2,1)S(1)}) fusion(f32[3,128,512]{1,2,0:T(8,128)S(1)} %multiply_add_fusion, f32[1,128,4,128]{1,3,2,0:T(8,128)S(1)} %get-tuple-element.51), kind=kLoop, calls=%fused_computation.80 | loop fusion | flops 524160 | bytes 1442304 | tf_op jit(solution)/shard_map/reduce_sum | solution.py:148
  27.3 1.6 %fusion.18 = f32[8,2,128,128]{3,0,2,1:T(8,128)} fusion(f32[1,128,8,128]{3,2,1,0:T(8,128)S(1)} %bitcast.169, f32[1,128,8,128]{3,2,1,0:T(8,128)S(1)} %copy.156), kind=kOutput, calls=%fused_computation.36 | convolution fusion | flops 12845952 | bytes 2097152 | tf_op jit(solution)/shard_map/...ab,ak->...kb/dot_general | solution.py:24
  28.9 1.6 %fusion.19 = f32[8,2,128,128]{3,0,2,1:T(8,128)} fusion(f32[1,128,8,128]{3,2,1,0:T(8,128)S(1)} %bitcast.170, f32[1,128,8,128]{3,2,1,0:T(8,128)S(1)} %copy.156), kind=kOutput, calls=%fused_computation.37 | convolution fusion | flops 12845952 | bytes 2097152 | tf_op jit(solution)/shard_map/...ab,ak->...kb/dot_general | solution.py:24
  30.5 1.1 %stack.58 = f32[2,128,1024]{1,2,0:T(8,128)} pad(f32[1,128,1024]{1,2,0:T(8,128)S(1)} %pad_bitcast_fusion, f32[]{:T(128)} %constant.67.clone.1), padding=0_1x0_0x0_0 | pad | bytes 1572868 | tf_op jit(solution)/shard_map/stack | solution.py:59
  31.6 1.6 %copy.158 = f32[2,128,8,128]{3,2,1,0:T(8,128)S(1)} copy(f32[2,128,8,128]{1,3,2,0:T(8,128)} %bitcast.176) | data formatting | bytes 2097152 | tf_op jit(solution)/shard_map/reshape | solution.py:38
  33.2 1.9 %convolution_add_fusion.3 = f32[8,2,128,128]{3,0,2,1:T(8,128)S(1)} fusion(f32[8,2,128,128]{3,0,2,1:T(8,128)} %fusion.18, f32[2,128,8,128]{3,2,1,0:T(8,128)S(1)} %copy.158), kind=kOutput, calls=%fused_computation.10 | convolution fusion | flops 12845952 | bytes 3145728 | tf_op jit(solution)/shard_map/...ab,ak->...kb/dot_general | solution.py:24
  35.2 0.8 add_bitcast_fusion.1
  36.0 0.9 fusion.12
  36.9 0.9 fusion.14
  37.8 0.9 fusion.3
  38.6 0.9 fusion.168
  39.5 0.3 copy.194
  39.8 0.9 slice.152
  40.7 0.5 slice_bitcast_fusion.1
  41.2 0.9 fusion.2
  42.2 0.3 copy.193
  42.5 0.8 slice.156
  43.3 0.5 slice_bitcast_fusion
  43.8 1.1 %copy.127 = f32[1,128,128,8]{1,3,2,0:T(8,128)} copy(f32[1,128,128,8]{1,2,3,0:T(8,128)S(1)} %get-tuple-element.45) | data formatting | bytes 1048576 | tf_op jit(solution)/shard_map/slice | solution.py:72
  44.9 1.3 %copy.128 = f32[1,128,8,128]{3,2,1,0:T(8,128)S(1)} copy(f32[1,128,8,128]{1,3,2,0:T(8,128)} %bitcast.187) | data formatting | bytes 1048576 | tf_op jit(solution)/shard_map/squeeze | solution.py:72
  46.2 2.2 %copy.119 = f32[1,128,128,8]{1,3,2,0:T(8,128)} copy(f32[1,128,128,8]{1,2,3,0:T(8,128)} %get-tuple-element.47) | data formatting | bytes 1048576 | tf_op jit(solution)/shard_map/slice | solution.py:71
  48.4 2.0 %copy.120 = f32[1,128,8,128]{3,2,1,0:T(8,128)} copy(f32[1,128,8,128]{1,3,2,0:T(8,128)} %bitcast.188) | data formatting | bytes 1048576 | tf_op jit(solution)/shard_map/squeeze | solution.py:71
  50.4 1.0 copy.118
  51.4 3.7 %slice.128 = f32[128,1023]{0,1:T(8,128)S(1)} reverse(f32[128,1023]{0,1:T(8,128)} %slice.152), dimensions={1} | reverse | bytes 1047552 | tf_op jit(solution)/shard_map/jit(_roll_static)/slice | solution.py:65
  55.2 1.5 %pad_maximum_fusion.12 = f32[1,128,1024]{1,2,0:T(8,128)} fusion(f32[1,128,1023]{1,2,0:T(8,128)S(1)} %bitcast.182, f32[1,128,1]{1,2,0:T(1,128)} %slice_bitcast_fusion.1), kind=kLoop, calls=%fused_computation.48 | loop fusion | flops 131072 | bytes 1048576 | tf_op jit(solution)/shard_map/jit(_roll_static)/concatenate | solution.py:65
  56.6 2.1 %copy.159 = f32[1,128,8,128]{3,2,1,0:T(8,128)} copy(f32[1,128,8,128]{1,3,2,0:T(8,128)} %bitcast.183) | data formatting | bytes 1048576 | tf_op jit(solution)/shard_map/jit(_roll_static)/concatenate | solution.py:65
  58.8 1.0 copy.126
  59.8 0.7 slice.133
  60.5 1.5 %pad_maximum_fusion.13 = f32[1,128,1024]{1,2,0:T(8,128)} fusion(f32[1,128,1023]{1,2,0:T(8,128)S(1)} %bitcast.184, f32[1,128,1]{1,2,0:T(1,128)} %slice_bitcast_fusion), kind=kLoop, calls=%fused_computation.49 | loop fusion | flops 131072 | bytes 1048576 | tf_op jit(solution)/shard_map/jit(_roll_static)/concatenate | solution.py:66
  62.1 2.1 %copy.160 = f32[1,128,8,128]{3,2,1,0:T(8,128)} copy(f32[1,128,8,128]{1,3,2,0:T(8,128)} %bitcast.185) | data formatting | bytes 1048576 | tf_op jit(solution)/shard_map/jit(_roll_static)/concatenate | solution.py:66
  64.2 1.6 %add_add_fusion = (f32[1,128,8,128]{3,2,1,0:T(8,128)S(1)}, f32[1,128,8,128]{3,2,1,0:T(8,128)S(1)}, f32[1,128,8,128]{3,2,1,0:T(8,128)S(1)}, f32[1,128,8,128]{3,2,1,0:T(8,128)S(1)}, f32[1,128,8,128]{3,2,1,0:T(8,128)S(1)}) fusion(f32[1,128,8,128]{3,2,1,0:T(8,128)S(1)} %copy.128, f32[1,128,8,128]{3,2,1,0:T(8,128)S(1)} %copy-done, ...), kind=kLoop, calls=%fused_computation.52 | loop fusion | flops 1966080 | bytes 5767168 | tf_op jit(solution)/shard_map/add | solution.py:80
  66.0 0.6 fusion.16
  66.7 0.6 fusion.17
  67.4 0.7 convolution_add_fusion.1
  68.0 0.9 add_bitcast_fusion
  68.9 0.9 fusion.8
  69.8 0.9 fusion.6
  70.7 0.9 fusion.1
  71.6 0.6 copy.191
  72.2 0.9 fusion
  73.1 0.6 copy.190
  74.5 1.5 %copy.143 = bf16[5,128,512]{1,0,2:T(8,128)(2,1)} copy(bf16[5,128,512]{1,2,0:T(8,128)(2,1)S(1)} %pad_maximum_fusion.11) | data formatting | bytes 1310720 | tf_op jit(solution)/shard_map/concatenate | solution.py:149
  76.0 3.6 %all-to-all-start.1 = ((bf16[5,128,512]{1,0,2:T(8,128)(2,1)}), bf16[5,128,512]{1,0,2:T(8,128)(2,1)S(1)}, u32[]{:S(2)}, u32[]{:S(2)}) async-start(bf16[5,128,512]{1,0,2:T(8,128)(2,1)} %copy.143), calls=%async_computation.1 | async-start | bytes 2097152 | tf_op jit(solution)/shard_map/all_to_all | solution.py:150
  79.8 15.3 %all_gather.6 = f32[3,512,3]{1,0,2:T(4,128)S(1)} all-gather(f32[3,128,3]{1,0,2:T(4,128)S(1)} %pad_maximum_fusion.14), channel_id=1, replica_groups=mesh['seq'=4,'chan'=8] {'seq'}, dimensions={1}, use_global_device_ids=true | all-gather | bytes 23040 | tf_op jit(solution)/shard_map/all_gather | solution.py:152
  95.1 0.6 copy.147
  95.7 5.0 %all-gather = f32[4,1,128]{2,1,0:T(1,128)S(1)} all-gather(f32[1,1,128]{2,1,0:T(1,128)S(1)} %bitcast.202), channel_id=1, replica_groups=mesh['seq'=4,'chan'=8] {'seq'}, dimensions={0}, use_global_device_ids=true | all-gather | bytes 2560 | tf_op jit(solution)/shard_map/all_gather | solution.py:153
  100.7 0.4 fusion.166
  101.1 0.3 slice.162
  101.4 0.8 copy.144
  102.2 1.0 copy.145
  103.2 0.8 copy.146
  104.0 0.6 copy.196
  (48 shorter events, 2.2 us)
Async XLA Ops:
  0.6 2.3 %copy-start.7 = (bf16[3,512,128]{2,1,0:T(8,128)(2,1)S(1)}, bf16[3,512,128]{2,1,0:T(8,128)(2,1)}, u32[]{:S(2)}) copy-start(bf16[3,512,128]{2,1,0:T(8,128)(2,1)} %param.5) | copy-start | bytes 1179652
  5.1 18.7 %all-to-all-start = ((bf16[5,512,128]{2,0,1:T(8,128)(2,1)}), bf16[5,512,128]{2,0,1:T(8,128)(2,1)S(1)}, u32[]{:S(2)}, u32[]{:S(2)}) async-start(bf16[5,512,128]{2,0,1:T(8,128)(2,1)} %pad_maximum_fusion), calls=%async_computation | async-start | bytes 2097152 | tf_op jit(solution)/shard_map/all_to_all | solution.py:132
  24.5 0.8 copy-start.1
  28.9 1.6 %copy-start.6 = (f32[128,512]{0,1:T(8,128)S(1)}, f32[128,512]{0,1:T(8,128)}, u32[]{:S(2)}) copy-start(f32[128,512]{0,1:T(8,128)} %get-tuple-element.23) | copy-start | bytes 786436
  33.2 2.0 %copy-start.3 = (f32[8,2,128,128]{3,0,2,1:T(8,128)S(1)}, f32[8,2,128,128]{3,0,2,1:T(8,128)}, u32[]{:S(2)}) copy-start(f32[8,2,128,128]{3,0,2,1:T(8,128)} %fusion.19) | copy-start | bytes 3145732
  33.2 2.0 %copy-start.9 = (f32[8,128]{1,0:T(8,128)S(1)}, f32[8,128]{1,0:T(8,128)}, u32[]{:S(2)}) copy-start(f32[8,128]{1,0:T(8,128)} %get-tuple-element.62) | copy-start | bytes 12292
  33.2 2.0 %copy-start.10 = (f32[8,128]{1,0:T(8,128)S(1)}, f32[8,128]{1,0:T(8,128)}, u32[]{:S(2)}) copy-start(f32[8,128]{1,0:T(8,128)} %get-tuple-element.63) | copy-start | bytes 12292
  56.6 3.1 %copy-start.4 = (f32[128,1023]{0,1:T(8,128)S(1)}, f32[128,1023]{0,1:T(8,128)}, u32[]{:S(2)}) copy-start(f32[128,1023]{0,1:T(8,128)} %slice.156) | copy-start | bytes 1571332
  60.5 3.7 %copy-start = (f32[1,128,8,128]{3,2,1,0:T(8,128)S(1)}, f32[1,128,8,128]{3,2,1,0:T(8,128)}, u32[]{:S(2)}) copy-start(f32[1,128,8,128]{3,2,1,0:T(8,128)} %copy.120) | copy-start | bytes 1572868
  62.1 2.1 %copy-start.5 = (f32[1,128,8,128]{3,2,1,0:T(8,128)S(1)}, f32[1,128,8,128]{3,2,1,0:T(8,128)}, u32[]{:S(2)}) copy-start(f32[1,128,8,128]{3,2,1,0:T(8,128)} %copy.118) | copy-start | bytes 1572868
  67.3 0.7 copy-start.8
  73.1 0.7 copy-start.12
  76.0 3.7 %copy-start.2 = (bf16[5,4,128,128]{2,3,1,0:T(8,128)(2,1)S(1)}, bf16[5,4,128,128]{2,3,1,0:T(8,128)(2,1)}, u32[]{:S(2)}) copy-start(bf16[5,4,128,128]{2,3,1,0:T(8,128)(2,1)} %copy-done.1) | copy-start | bytes 1966084
  76.0 24.7 %all-to-all-start.1 = ((bf16[5,128,512]{1,0,2:T(8,128)(2,1)}), bf16[5,128,512]{1,0,2:T(8,128)(2,1)S(1)}, u32[]{:S(2)}, u32[]{:S(2)}) async-start(bf16[5,128,512]{1,0,2:T(8,128)(2,1)} %copy.143), calls=%async_computation.1 | async-start | bytes 2097152 | tf_op jit(solution)/shard_map/all_to_all | solution.py:150
  79.6 16.0 %copy-start.11 = (f32[128]{0:T(128)S(1)}, f32[128]{0:T(128)}, u32[]{:S(2)}) copy-start(f32[128]{0:T(128)} %get-tuple-element.22) | copy-start | bytes 1540
where the time goes:
time: 105 us
  local copies, waits for them, and re-layouts  38.1 us (36%)
  blocking collectives  20.3 us (19%)
  matrix products  15.7 us (15%)
  waiting for transfers between devices  10.9 us (10%)
  other arithmetic  10.6 us (10%)
  starting transfers between devices  7.88 us (8%)
  between operations  1.1 us (1%)
    all_gather x1, blocking collectives, shards(): lax.all_gather(taps_grad, 'seq', axis=1, tiled=True)  15.3 us
    all_to_all x1, waiting for transfers between devices, shards(): lax.all_to_all(stacked, 'seq', split_axis=1, concat_axis=2, tiled=True)  10.9 us
    dot_general x8, matrix products, first_axis(): jnp.einsum('...ab,ak->...kb', operand, matrix, precision=lax.Precision.HIGH)  8.77 us
    dot_general x8, matrix products, last_axis(): jnp.einsum('...n,nk->...k', operand, matrix, precision=lax.Precision.HIGH)  6.96 us
    all_gather x1, blocking collectives, shards(): lax.all_gather(gain_grad, 'seq', axis=0, tiled=True)  5.05 us
    slice x2, local copies, waits for them, and re-layouts, spectral(): mirror_real = jnp.roll(jnp.flip(packed_real, -1), 1, -1)  4.57 us
    all_to_all x1, starting transfers between devices, shards(): lax.all_to_all(stacked, 'seq', split_axis=1, concat_axis=2, tiled=True)  4.24 us
    all_to_all x1, starting transfers between devices, shards(): lax.all_to_all(results, 'seq', split_axis=2, concat_axis=1, tiled=True)  3.65 us
  transfers between devices with their start and end apart: 2, of which 1 were waited for; matrix products, arithmetic and copies ran while one was open for 4% of the time, Pallas kernels for 0%

commit v1 on v0

--- a/solution.py
+++ b/solution.py
@@ -129,7 +129,10 @@
     margin = short_filters.shape[2] - 1
     local_gain = lax.dynamic_slice_in_dim(skip_gain, seq_index * per_group, per_group, 0)
     stacked = jnp.concatenate([features, cotangent[None], long_filter[None]], 0)
-    columns = lax.all_to_all(stacked, "seq", split_axis=1, concat_axis=2, tiled=True)
+    columns = jnp.concatenate(
+        lax.all_to_all(jnp.stack(jnp.split(stacked, lax.axis_size("seq"), axis=1)), "seq", 0, 0),
+        axis=2,
+    )
     weights = lax.dynamic_slice_in_dim(short_filters, seq_index * per_group, per_group, 1)
     length = columns.shape[2]
     history = jnp.pad(columns[:3].astype(jnp.float32), ((0, 0), (0, 0), (margin, 0)))

time: 105 us -> 100 us (0.952)
  waiting for transfers between devices: 10.9 us -> 6.74 us
  other arithmetic: 10.6 us -> 8.34 us
    all_to_all x1, waiting for transfers between devices: 10.9 us -> 6.74 us  [shards(): lax.all_to_all(jnp.stack(jnp.split(stacked, lax.axis_size('seq'), axis=1)...]
    unnamed x32 -> x39, local copies, waits for them, and re-layouts: 2.35 us -> 5.95 us
    broadcast_in_dim x2 -> x0, local copies, waits for them, and re-layouts: 2.27 us -> none  [shards(): stacked = jnp.concatenate([features, cotangent[None], long_filter[None]], 0)]
    concatenate x1, other arithmetic: 1.87 us -> 0.08 us  [shards(): stacked = jnp.concatenate([features, cotangent[None], long_filter[None]], 0)]
where the time goes in v1:
time: 100 us; the launch traced here: 99.1 us
  local copies, waits for them, and re-layouts  38.9 us (39%)
  blocking collectives  20.3 us (20%)
  matrix products  15.7 us (16%)
  other arithmetic  8.34 us (8%)
  starting transfers between devices  7.88 us (8%)
  waiting for transfers between devices  6.74 us (7%)
  between operations  1.13 us (1%)
    all_gather x1, blocking collectives, shards(): lax.all_gather(taps_grad, 'seq', axis=1, tiled=True)  15.3 us
    dot_general x8, matrix products, first_axis(): jnp.einsum('...ab,ak->...kb', operand, matrix, precision=lax.Precision.HIGH)  8.76 us
    dot_general x8, matrix products, last_axis(): jnp.einsum('...n,nk->...k', operand, matrix, precision=lax.Precision.HIGH)  6.96 us
    all_to_all x1, waiting for transfers between devices, shards(): lax.all_to_all(jnp.stack(jnp.split(stacked, lax.axis_size('seq'), axis=1)...  6.74 us
    unnamed x39, local copies, waits for them, and re-layouts  5.95 us
    all_gather x1, blocking collectives, shards(): lax.all_gather(gain_grad, 'seq', axis=0, tiled=True)  5.05 us
    slice x2, local copies, waits for them, and re-layouts, spectral(): mirror_real = jnp.roll(jnp.flip(packed_real, -1), 1, -1)  4.55 us
    all_to_all x1, starting transfers between devices, shards(): lax.all_to_all(jnp.stack(jnp.split(stacked, lax.axis_size('seq'), axis=1)...  4.24 us
  transfers between devices with their start and end apart: 2, of which 1 were waited for; matrix products, arithmetic and copies ran while one was open for 4% of the time, Pallas kernels for 0%

profile of v1, /device:TPU:0, one launch (start us, length us, event | category | flops | bytes accessed | tf_op | source)
XLA Modules:
  0.0 99.1 jit_solution(103293544028999403)
XLA Ops:
  0.7 1.1 %copy.65 = bf16[512,128]{0,1:T(8,128)(2,1)S(1)} copy(bf16[512,128]{1,0:T(8,128)(2,1)} %param.7) | data formatting | bytes 262144 | tf_op args[2]
  2.3 0.9 pad_maximum_fusion.11
  3.3 4.2 %all-to-all-start = ((bf16[4,5,128,128]{2,3,1,0:T(8,128)(2,1)}), bf16[4,5,128,128]{2,3,1,0:T(8,128)(2,1)S(1)}, u32[]{:S(2)}, u32[]{:S(2)}) async-start(bf16[4,5,128,128]{2,3,1,0:T(8,128)(2,1)} %pad_maximum_fusion.11), calls=%async_computation | async-start | bytes 1310720 | tf_op jit(solution)/shard_map/all_to_all | solution.py:133
  7.5 0.9 constant_dynamic-slice_fusion.1
  8.4 1.3 %dynamic_slice.7 = f32[128]{0:T(128)} dynamic-slice(f32[512]{0:T(512)} %param.9, s32[]{:T(128)S(6)} %select_n.84), dynamic_slice_sizes={128} | dynamic-slice | bytes 1028 | tf_op jit(solution)/shard_map/dynamic_slice | solution.py:130
  9.7 0.7 multiply_sine_fusion.7
  10.3 0.6 multiply_sine_fusion.6
  11.0 6.7 %all-to-all-done = bf16[4,5,128,128]{2,3,1,0:T(8,128)(2,1)S(1)} async-done(((bf16[4,5,128,128]{2,3,1,0:T(8,128)(2,1)}), bf16[4,5,128,128]{2,3,1,0:T(8,128)(2,1)S(1)}, u32[]{:S(2)}, u32[]{:S(2)}) %all-to-all-start) | async-done | bytes 655392 | tf_op jit(solution)/shard_map/all_to_all | solution.py:133
  17.9 0.7 copy-done.1
  19.1 1.3 %multiply_reduce_fusion.2 = (f32[128]{0:T(128)}, f32[128,512]{0,1:T(8,128)}, bf16[1,128,512]{1,2,0:T(8,128)(2,1)S(1)}) fusion(f32[3,128,512]{1,2,0:T(8,128)S(1)} %multiply_add_fusion, f32[1,128,4,128]{1,3,2,0:T(8,128)S(1)} %get-tuple-element.46), kind=kLoop, calls=%fused_computation.81 | loop fusion | flops 524160 | bytes 1442304 | tf_op jit(solution)/shard_map/reduce_sum | solution.py:151
  20.7 1.6 %fusion.18 = f32[8,2,128,128]{3,0,2,1:T(8,128)} fusion(f32[1,128,8,128]{3,2,1,0:T(8,128)S(1)} %copy.115, f32[1,128,8,128]{3,2,1,0:T(8,128)S(1)} %copy.114), kind=kOutput, calls=%fused_computation.35 | convolution fusion | flops 12845952 | bytes 2097152 | tf_op jit(solution)/shard_map/...ab,ak->...kb/dot_general | solution.py:24
  22.3 1.6 %fusion.19 = f32[8,2,128,128]{3,0,2,1:T(8,128)} fusion(f32[1,128,8,128]{3,2,1,0:T(8,128)S(1)} %copy.115, f32[1,128,8,128]{3,2,1,0:T(8,128)S(1)} %copy.114), kind=kOutput, calls=%fused_computation.36 | convolution fusion | flops 12845952 | bytes 2097152 | tf_op jit(solution)/shard_map/...ab,ak->...kb/dot_general | solution.py:24
  23.9 1.1 %stack.78 = f32[2,128,1024]{1,2,0:T(8,128)} pad(f32[1,128,1024]{1,2,0:T(8,128)S(1)} %pad_bitcast_fusion, f32[]{:T(128)} %constant.67.clone.1), padding=0_1x0_0x0_0 | pad | bytes 1572868 | tf_op jit(solution)/shard_map/stack | solution.py:59
  25.0 1.6 %copy.116 = f32[2,128,8,128]{3,2,1,0:T(8,128)S(1)} copy(f32[2,128,8,128]{1,3,2,0:T(8,128)} %bitcast.181) | data formatting | bytes 2097152 | tf_op jit(solution)/shard_map/reshape | solution.py:38
  26.6 1.9 %convolution_add_fusion.3 = f32[8,2,128,128]{3,0,2,1:T(8,128)S(1)} fusion(f32[8,2,128,128]{3,0,2,1:T(8,128)} %fusion.18, f32[2,128,8,128]{3,2,1,0:T(8,128)S(1)} %copy.116), kind=kOutput, calls=%fused_computation.10 | convolution fusion | flops 12845952 | bytes 3145728 | tf_op jit(solution)/shard_map/...ab,ak->...kb/dot_general | solution.py:24
  28.6 0.8 add_bitcast_fusion.1
  29.4 0.9 fusion.12
  30.3 0.9 fusion.14
  31.1 0.9 fusion.3
  32.0 0.9 fusion.168
  32.9 0.3 copy.153
  33.2 0.8 slice.152
  34.1 0.5 slice_bitcast_fusion.5
  34.6 0.9 fusion.2
  35.5 0.3 copy.152
  35.9 0.8 slice.156
  36.7 0.5 slice_bitcast_fusion.4
  37.2 1.1 %copy.85 = f32[1,128,128,8]{1,3,2,0:T(8,128)} copy(f32[1,128,128,8]{1,2,3,0:T(8,128)S(1)} %get-tuple-element.40) | data formatting | bytes 1048576 | tf_op jit(solution)/shard_map/slice | solution.py:72
  38.3 1.3 %copy.86 = f32[1,128,8,128]{3,2,1,0:T(8,128)S(1)} copy(f32[1,128,8,128]{1,3,2,0:T(8,128)} %bitcast.191) | data formatting | bytes 1048576 | tf_op jit(solution)/shard_map/squeeze | solution.py:72
  39.6 2.1 %copy.77 = f32[1,128,128,8]{1,3,2,0:T(8,128)} copy(f32[1,128,128,8]{1,2,3,0:T(8,128)} %get-tuple-element.42) | data formatting | bytes 1048576 | tf_op jit(solution)/shard_map/slice | solution.py:71
  41.7 2.1 %copy.78 = f32[1,128,8,128]{3,2,1,0:T(8,128)} copy(f32[1,128,8,128]{1,3,2,0:T(8,128)} %bitcast.192) | data formatting | bytes 1048576 | tf_op jit(solution)/shard_map/squeeze | solution.py:71
  43.8 1.0 %copy.76 = f32[1,128,8,128]{3,2,1,0:T(8,128)} copy(f32[1,128,8,128]{1,3,2,0:T(8,128)S(1)} %bitcast.172) | data formatting | bytes 1048576 | tf_op jit(solution)/shard_map/squeeze | solution.py:63
  44.8 3.7 %slice.128 = f32[128,1023]{0,1:T(8,128)S(1)} reverse(f32[128,1023]{0,1:T(8,128)} %slice.152), dimensions={1} | reverse | bytes 1047552 | tf_op jit(solution)/shard_map/jit(_roll_static)/slice | solution.py:65
  48.5 0.6 copy-done.13
  49.2 0.8 pad_maximum_fusion.13
  50.0 2.0 %copy.117 = f32[1,128,8,128]{3,2,1,0:T(8,128)} copy(f32[1,128,8,128]{1,3,2,0:T(8,128)} %bitcast.187) | data formatting | bytes 1048576 | tf_op jit(solution)/shard_map/jit(_roll_static)/concatenate | solution.py:65
  52.0 1.0 %copy.84 = f32[1,128,8,128]{3,2,1,0:T(8,128)} copy(f32[1,128,8,128]{1,3,2,0:T(8,128)S(1)} %bitcast.175) | data formatting | bytes 1048576 | tf_op jit(solution)/shard_map/squeeze | solution.py:64
  53.1 0.7 slice.133
  53.8 0.6 copy-done.14
  54.4 0.8 pad_maximum_fusion.14
  55.3 2.1 %copy.118 = f32[1,128,8,128]{3,2,1,0:T(8,128)} copy(f32[1,128,8,128]{1,3,2,0:T(8,128)} %bitcast.189) | data formatting | bytes 1048576 | tf_op jit(solution)/shard_map/jit(_roll_static)/concatenate | solution.py:66
  57.4 1.6 %add_add_fusion = (f32[1,128,8,128]{3,2,1,0:T(8,128)S(1)}, f32[1,128,8,128]{3,2,1,0:T(8,128)S(1)}, f32[1,128,8,128]{3,2,1,0:T(8,128)S(1)}, f32[1,128,8,128]{3,2,1,0:T(8,128)S(1)}, f32[1,128,8,128]{3,2,1,0:T(8,128)S(1)}) fusion(f32[1,128,8,128]{3,2,1,0:T(8,128)S(1)} %copy.86, f32[1,128,8,128]{3,2,1,0:T(8,128)S(1)} %copy-done, ...), kind=kLoop, calls=%fused_computation.53 | loop fusion | flops 1966080 | bytes 5767168 | tf_op jit(solution)/shard_map/add | solution.py:80
  59.3 0.6 fusion.16
  59.9 0.6 fusion.17
  60.6 0.7 convolution_add_fusion.1
  61.3 0.9 add_bitcast_fusion
  62.2 0.9 fusion.8
  63.1 0.9 fusion.6
  64.0 0.9 fusion.1
  64.8 0.6 copy.149
  65.4 0.9 fusion
  66.3 0.6 copy.148
  67.0 0.6 copy-done.15
  68.4 1.5 %copy.101 = bf16[5,128,512]{1,0,2:T(8,128)(2,1)} copy(bf16[5,128,512]{1,2,0:T(8,128)(2,1)S(1)} %pad_maximum_fusion.12) | data formatting | bytes 1310720 | tf_op jit(solution)/shard_map/concatenate | solution.py:152
  69.8 3.6 %all-to-all-start.1 = ((bf16[5,128,512]{1,0,2:T(8,128)(2,1)}), bf16[5,128,512]{1,0,2:T(8,128)(2,1)S(1)}, u32[]{:S(2)}, u32[]{:S(2)}) async-start(bf16[5,128,512]{1,0,2:T(8,128)(2,1)} %copy.101), calls=%async_computation.1 | async-start | bytes 2097152 | tf_op jit(solution)/shard_map/all_to_all | solution.py:153
  73.6 15.3 %all_gather.6 = f32[3,512,3]{1,0,2:T(4,128)S(1)} all-gather(f32[3,128,3]{1,0,2:T(4,128)S(1)} %pad_maximum_fusion.15), channel_id=1, replica_groups=mesh['seq'=4,'chan'=8] {'seq'}, dimensions={1}, use_global_device_ids=true | all-gather | bytes 23040 | tf_op jit(solution)/shard_map/all_gather | solution.py:155
  88.9 0.6 copy.105
  89.5 0.7 copy-done.12
  90.2 5.0 %all-gather = f32[4,1,128]{2,1,0:T(1,128)S(1)} all-gather(f32[1,1,128]{2,1,0:T(1,128)S(1)} %bitcast.207), channel_id=1, replica_groups=mesh['seq'=4,'chan'=8] {'seq'}, dimensions={0}, use_global_device_ids=true | all-gather | bytes 2560 | tf_op jit(solution)/shard_map/all_gather | solution.py:156
  95.2 0.4 fusion.166
  95.9 0.8 copy.102
  96.7 1.0 %copy.103 = bf16[3,4,128,128]{3,2,1,0:T(8,128)(2,1)} copy(bf16[3,4,128,128]{2,0,3,1:T(4,128)(2,1)S(1)} %slice.162) | data formatting | bytes 786432 | tf_op jit(solution)/shard_map/slice | solution.py:158
  97.7 0.8 copy.104
  98.5 0.6 copy.155
  (55 shorter events, 3.0 us)
Async XLA Ops:
  0.6 1.1 %copy-start.8 = (bf16[512,128]{1,0:T(8,128)(2,1)S(1)}, bf16[512,128]{1,0:T(8,128)(2,1)}, u32[]{:S(2)}) copy-start(bf16[512,128]{1,0:T(8,128)(2,1)} %param.6) | copy-start | bytes 393220
  0.6 1.2 %copy-start.7 = (bf16[3,512,128]{2,1,0:T(8,128)(2,1)S(1)}, bf16[3,512,128]{2,1,0:T(8,128)(2,1)}, u32[]{:S(2)}) copy-start(bf16[3,512,128]{2,1,0:T(8,128)(2,1)} %param.5) | copy-start | bytes 1179652
  3.3 14.5 %all-to-all-start = ((bf16[4,5,128,128]{2,3,1,0:T(8,128)(2,1)}), bf16[4,5,128,128]{2,3,1,0:T(8,128)(2,1)S(1)}, u32[]{:S(2)}, u32[]{:S(2)}) async-start(bf16[4,5,128,128]{2,3,1,0:T(8,128)(2,1)} %pad_maximum_fusion.11), calls=%async_computation | async-start | bytes 1310720 | tf_op jit(solution)/shard_map/all_to_all | solution.py:133
  17.8 0.8 copy-start.1
  22.3 1.6 %copy-start.6 = (f32[128,512]{0,1:T(8,128)S(1)}, f32[128,512]{0,1:T(8,128)}, u32[]{:S(2)}) copy-start(f32[128,512]{0,1:T(8,128)} %get-tuple-element.18) | copy-start | bytes 786436
  26.6 2.0 %copy-start.3 = (f32[8,2,128,128]{3,0,2,1:T(8,128)S(1)}, f32[8,2,128,128]{3,0,2,1:T(8,128)}, u32[]{:S(2)}) copy-start(f32[8,2,128,128]{3,0,2,1:T(8,128)} %fusion.19) | copy-start | bytes 3145732
  26.6 2.0 %copy-start.10 = (f32[8,128]{1,0:T(8,128)S(1)}, f32[8,128]{1,0:T(8,128)}, u32[]{:S(2)}) copy-start(f32[8,128]{1,0:T(8,128)} %get-tuple-element.61) | copy-start | bytes 12292
  26.6 2.0 %copy-start.11 = (f32[8,128]{1,0:T(8,128)S(1)}, f32[8,128]{1,0:T(8,128)}, u32[]{:S(2)}) copy-start(f32[8,128]{1,0:T(8,128)} %get-tuple-element.62) | copy-start | bytes 12292
  48.5 0.7 copy-start.13
  52.0 1.0 %copy-start.4 = (f32[128,1023]{0,1:T(8,128)S(1)}, f32[128,1023]{0,1:T(8,128)}, u32[]{:S(2)}) copy-start(f32[128,1023]{0,1:T(8,128)} %slice.156) | copy-start | bytes 1571332
  53.8 0.7 copy-start.14
  55.3 2.1 %copy-start = (f32[1,128,8,128]{3,2,1,0:T(8,128)S(1)}, f32[1,128,8,128]{3,2,1,0:T(8,128)}, u32[]{:S(2)}) copy-start(f32[1,128,8,128]{3,2,1,0:T(8,128)} %copy.78) | copy-start | bytes 1572868
  55.3 2.1 %copy-start.5 = (f32[1,128,8,128]{3,2,1,0:T(8,128)S(1)}, f32[1,128,8,128]{3,2,1,0:T(8,128)}, u32[]{:S(2)}) copy-start(f32[1,128,8,128]{3,2,1,0:T(8,128)} %copy.76) | copy-start | bytes 1572868
  60.6 0.7 copy-start.9
  66.9 0.6 copy-start.15
  69.8 3.7 %copy-start.2 = (bf16[4,5,128,128]{2,3,0,1:T(8,128)(2,1)S(1)}, bf16[4,5,128,128]{2,3,0,1:T(8,128)(2,1)}, u32[]{:S(2)}) copy-start(bf16[4,5,128,128]{2,3,0,1:T(8,128)(2,1)} %copy-done.1) | copy-start | bytes 1966084
  69.8 25.4 %all-to-all-start.1 = ((bf16[5,128,512]{1,0,2:T(8,128)(2,1)}), bf16[5,128,512]{1,0,2:T(8,128)(2,1)S(1)}, u32[]{:S(2)}, u32[]{:S(2)}) async-start(bf16[5,128,512]{1,0,2:T(8,128)(2,1)} %copy.101), calls=%async_computation.1 | async-start | bytes 2097152 | tf_op jit(solution)/shard_map/all_to_all | solution.py:153
  89.5 0.7 copy-start.12
